TPU v7x, 1024 devices: a whole 4x8x16 slice. The times are simulated.
1024 devices in a mesh: pipe: 16 (over z), expert: 64 (over x, y, core).
Axes of the slice: x: 4, y: 8, z: 16, core: 2. Of those that a mesh axis runs over, the one named last changes fastest.
Arguments:
- up_state: bfloat16 [16, 2048, 3584], P('pipe', 'expert'), may hold values from -6 to 6
- down_state: bfloat16 [16, 2048, 3584], P('pipe', 'expert'), may hold values from -6 to 6
- entering: bfloat16 [2, 1, 2048, 3584], P(None, None, 'expert'), may hold values from -6 to 6
- norm_gain: float32 [16, 3584], P('pipe'), may hold values from 0.1 to 1.9
- router: bfloat16 [16, 3584, 32], P('pipe'), may hold values from -0.09375 to 0.09375
- routes: int32 [16, 2, 64, 64, 1], P('pipe', None, 'expert'), may hold values from 0 to 31; in each aligned block of 64 rows (0 to 63, 64 to 127, ..., all dimensions but the last counted through in order) at most 4 rows name the same one
- w_in: bfloat16 [3584, 32768], P(None, 'expert'), may hold values from -0.09375 to 0.09375
- w_out: bfloat16 [32768, 3584], P('expert'), may hold values from -0.1875 to 0.1875
Outputs:
- up_out: bfloat16 [16, 2048, 3584], P('pipe', 'expert')
- down_out: bfloat16 [16, 2048, 3584], P('pipe', 'expert')
Inputs may be any that keep to these rules, and one draw needn't show every extreme that they name: `routes`: the 1 ids of a row are distinct. Among the 64 rows of one index of expert at one section and step, no expert is chosen more than 4 times, and some expert is chosen exactly 4 times.
All inputs are finite; a program needn't handle non-finite values.
Results may differ from a plain program's by a relative error of at most 0.0067.
Values may be sent and summed in bfloat16 or wider, within the bound.
A program may use at most 32 MiB of HBM per device.

v0:
```python
import jax
import jax.numpy as jnp
from jax import lax
from jax.sharding import PartitionSpec as P

TOPK = 1
STEPS = 2


ROUTE_SCALE = 2.5
NORM_EPS = 1e-06


def from_behind(value, axis, steps):
    count = lax.axis_size(axis)
    leading, last = (max(0, -steps), min(count, count - steps))
    return lax.ppermute(value, axis, [(source, source + steps) for source in range(leading, last)])


def normalize(row_block, gain_row):
    values = row_block.astype(jnp.float32)
    square = jnp.mean(values * values, axis=-1, keepdims=True)
    return (values * lax.rsqrt(square + NORM_EPS) * gain_row).astype(jnp.bfloat16)


def expert_part(arrived_rows, w_in, w_out):
    hidden = jax.nn.silu(jnp.dot(arrived_rows, w_in, preferred_element_type=jnp.float32)).astype(
        jnp.bfloat16
    )
    return jnp.dot(hidden, w_out, preferred_element_type=jnp.float32).astype(jnp.bfloat16)


def layer_rows(row_block, gain_row, router_cols, row_ids, w_in, w_out):
    row_count, width = row_block.shape
    expert_count = router_cols.shape[1]
    holder_count = lax.axis_size("expert")
    capacity = 2 * row_count * TOPK // expert_count
    normed = normalize(row_block, gain_row)
    scores = jax.nn.sigmoid(jnp.dot(normed, router_cols, preferred_element_type=jnp.float32))
    gate_items = (ROUTE_SCALE * jnp.take_along_axis(scores, row_ids, axis=1)).reshape(-1)
    item_ids = row_ids.reshape(-1)
    piece_count = item_ids.shape[0]
    member = (item_ids[:, None] == jnp.arange(expert_count, dtype=jnp.int32)[None, :]).astype(
        jnp.int32
    )
    rank_table = jnp.cumsum(member, axis=0) - 1
    item_rank = jnp.sum(rank_table * member, axis=1)
    item_slot = item_ids * capacity + item_rank
    picked = (
        jnp.zeros((expert_count * capacity,), jnp.int32)
        .at[item_slot]
        .set(jnp.arange(piece_count, dtype=jnp.int32))
    )
    live_slot = jnp.zeros((expert_count * capacity,), jnp.bool_).at[item_slot].set(True)
    send_block = jnp.where(live_slot[:, None], normed[picked // TOPK], jnp.zeros((), jnp.bfloat16))
    send_block = send_block.reshape(expert_count, capacity, width)
    outgoing = jnp.broadcast_to(send_block[:, None], (expert_count, 2, capacity, width)).reshape(
        holder_count, capacity, width
    )
    arrived = lax.all_to_all(outgoing, "expert", split_axis=0, concat_axis=0, tiled=True)
    partial_value = expert_part(arrived.reshape(holder_count * capacity, width), w_in, w_out)
    returned = lax.all_to_all(
        partial_value.reshape(holder_count, capacity, width),
        "expert",
        split_axis=0,
        concat_axis=0,
        tiled=True,
    )
    paired = returned.reshape(expert_count, 2, capacity, width)
    summed = (paired[:, 0].astype(jnp.float32) + paired[:, 1].astype(jnp.float32)).reshape(
        expert_count * capacity, width
    )
    item_out = summed[item_slot] * gate_items[:, None]
    moe_total = jnp.sum(item_out.reshape(row_count, TOPK, width), axis=1)
    return (row_block.astype(jnp.float32) + moe_total).astype(jnp.bfloat16)


def shards(up_state, down_state, entering, norm_gain, router, routes, w_in, w_out):
    section_index = lax.axis_index("pipe")
    last_section = lax.axis_size("pipe") - 1
    gain_row = norm_gain[0]
    router_cols = router[0]
    upward = up_state[0]
    downward = down_state[0]
    tok_count = upward.shape[0]
    up_new = upward
    down_new = downward
    for step_idx in range(STEPS):
        row_block = jnp.concatenate([upward, downward], axis=0)
        advanced = layer_rows(row_block, gain_row, router_cols, routes[0, step_idx, 0], w_in, w_out)
        up_new = advanced[:tok_count]
        down_new = advanced[tok_count:]
        if step_idx + 1 < STEPS:
            moved_up = from_behind(up_new, "pipe", 1)
            moved_down = from_behind(down_new, "pipe", -1)
            upward = jnp.where(section_index == 0, entering[0, step_idx], moved_up)
            downward = jnp.where(section_index == last_section, entering[1, step_idx], moved_down)
    return (up_new[None], down_new[None])


def solution(mesh):
    return jax.shard_map(
        shards,
        mesh=mesh,
        in_specs=(
            P("pipe", "expert", None),
            P("pipe", "expert", None),
            P(None, None, "expert", None),
            P("pipe", None),
            P("pipe", None, None),
            P("pipe", None, "expert", None, None),
            P(None, "expert"),
            P("expert", None),
        ),
        out_specs=(P("pipe", "expert", None), P("pipe", "expert", None)),
        check_vma=False,
    )
```

profile of v0, /device:TPU:1, one launch (start us, length us, event | category | flops | bytes accessed | tf_op | source)
XLA Modules:
  0.0 268.4 jit_solution(6080947441183881807)
XLA Ops:
  0.6 0.0 copy-start
  0.6 1.3 fusion.6
  1.9 0.7 slice_bitcast_fusion.6
  2.6 0.1 fusion.18
  2.7 0.1 fusion.19
  2.8 0.1 reduce_window_sum.18
  2.9 0.1 reduce_window_sum.17
  3.0 0.2 select_reduce_fusion
  3.1 0.7 fusion.35
  3.8 0.8 scatter_custom_fusion.1
  4.6 0.8 scatter_custom_fusion
  5.4 0.1 broadcast_in_dim.59
  5.6 0.8 reduce
  6.3 1.2 fusion.8
  7.5 1.1 gather_fusion
  8.7 0.2 gather.20
  8.9 0.5 broadcast_select_fusion.1
  9.4 0.5 broadcast_in_dim.63
  9.9 62.8 %all_to_all.20 = bf16[64,4,3584]{2,1,0:T(4,128)(2,1)S(1)} all-to-all(bf16[64,4,3584]{2,1,0:T(4,128)(2,1)S(1)} %bitcast.111), channel_id=1, replica_groups=mesh['pipe'=16,'expert'=64] {'expert'}, dimensions={0} | all-to-all | bytes 3670016 | tf_op jit(solution)/shard_map/all_to_all | solution.py:60
  72.7 1.5 reshape.171
  74.2 5.9 %convolution_convert_fusion.1 = bf16[256,3584]{1,0:T(8,128)(2,1)S(1)} fusion(bf16[512,3584]{1,0:T(8,128)(2,1)} %param.17, bf16[256,3584]{1,0:T(8,128)(2,1)} %reshape.171, bf16[3584,512]{1,0:T(8,128)(2,1)} %param.16), kind=kOutput, calls=%fused_computation.11 | convolution fusion | flops 1880621056 | bytes 11010048 | tf_op jit(solution)/shard_map/dot_general | solution.py:30
  80.1 1.5 reshape.172
  81.6 0.0 copy-start.4
  81.6 6.2 %all-to-all-start.1 = ((bf16[64,4,3584]{2,1,0:T(4,128)(2,1)}), bf16[64,4,3584]{2,1,0:T(4,128)(2,1)S(1)}, u32[]{:S(2)}, u32[]{:S(2)}) async-start(bf16[64,4,3584]{2,1,0:T(4,128)(2,1)} %reshape.172), calls=%async_computation.1 | async-start | bytes 3670016 | tf_op jit(solution)/shard_map/all_to_all | solution.py:62
  87.8 0.8 scatter_custom_fusion.2
  88.6 0.8 scatter_custom_fusion.3
  89.3 0.1 broadcast_in_dim.64
  89.5 0.0 copy-done
  89.5 0.3 fusion.5
  89.8 0.8 gather_fusion.4
  90.6 0.0 copy-done.4
  90.6 42.5 %all-to-all-done.1 = bf16[64,4,3584]{2,1,0:T(4,128)(2,1)S(1)} async-done(((bf16[64,4,3584]{2,1,0:T(4,128)(2,1)}), bf16[64,4,3584]{2,1,0:T(4,128)(2,1)S(1)}, u32[]{:S(2)}, u32[]{:S(2)}) %all-to-all-start.1) | async-done | bytes 1835040 | tf_op jit(solution)/shard_map/all_to_all | solution.py:62
  133.1 1.7 convert_add_fusion.1
  134.8 1.9 add.115
  136.8 0.0 copy-start.1
  136.8 0.0 copy-start.2
  136.8 0.9 gather_fusion.1
  137.7 0.0 copy-done.1
  137.7 0.1 copy-done.2
  137.9 0.2 fusion.9
  138.1 1.3 collective-permute-start
  139.4 1.5 collective-permute-start.1
  140.9 3.3 %collective-permute-done = bf16[32,3584]{1,0:T(8,128)(2,1)S(1)} collective-permute-done((bf16[32,3584]{1,0:T(8,128)(2,1)S(1)}, bf16[32,3584]{1,0:T(8,128)(2,1)S(1)}, u32[]{:S(2)}, u32[]{:S(2)}) %collective-permute-start) | collective-permute-done | bytes 229408 | tf_op jit(solution)/shard_map/ppermute | solution.py:17
  144.2 3.8 %collective-permute-done.1 = bf16[32,3584]{1,0:T(8,128)(2,1)S(1)} collective-permute-done((bf16[32,3584]{1,0:T(8,128)(2,1)S(1)}, bf16[32,3584]{1,0:T(8,128)(2,1)S(1)}, u32[]{:S(2)}, u32[]{:S(2)}) %collective-permute-start.1) | collective-permute-done | bytes 229408 | tf_op jit(solution)/shard_map/ppermute | solution.py:17
  148.1 0.0 copy-done.3
  148.1 0.2 fusion.10
  148.3 0.2 fusion.12
  148.5 1.1 gather_fusion.2
  149.6 0.2 gather.23
  149.9 0.5 broadcast_select_fusion
  150.3 0.5 broadcast_in_dim.67
  150.8 51.8 %all_to_all.21 = bf16[64,4,3584]{2,1,0:T(4,128)(2,1)S(1)} all-to-all(bf16[64,4,3584]{2,1,0:T(4,128)(2,1)S(1)} %bitcast.112), channel_id=1, replica_groups=mesh['pipe'=16,'expert'=64] {'expert'}, dimensions={0} | all-to-all | bytes 3670016 | tf_op jit(solution)/shard_map/all_to_all | solution.py:60
  202.6 1.5 reshape.175
  204.1 5.9 %convolution_convert_fusion = bf16[256,3584]{1,0:T(8,128)(2,1)S(1)} fusion(bf16[512,3584]{1,0:T(8,128)(2,1)} %param.17, bf16[256,3584]{1,0:T(8,128)(2,1)} %reshape.175, bf16[3584,512]{1,0:T(8,128)(2,1)} %param.16), kind=kOutput, calls=%fused_computation.10 | convolution fusion | flops 1880621056 | bytes 11010048 | tf_op jit(solution)/shard_map/dot_general | solution.py:30
  210.0 1.5 reshape.176
  211.5 6.0 %all-to-all-start.3 = ((bf16[64,4,3584]{2,1,0:T(4,128)(2,1)}), bf16[64,4,3584]{2,1,0:T(4,128)(2,1)S(1)}, u32[]{:S(2)}, u32[]{:S(2)}) async-start(bf16[64,4,3584]{2,1,0:T(4,128)(2,1)} %reshape.176), calls=%async_computation.3 | async-start | bytes 3670016 | tf_op jit(solution)/shard_map/all_to_all | solution.py:62
  217.5 0.3 fusion.2
  217.8 0.8 gather_fusion.5
  218.6 44.3 %all-to-all-done.3 = bf16[64,4,3584]{2,1,0:T(4,128)(2,1)S(1)} async-done(((bf16[64,4,3584]{2,1,0:T(4,128)(2,1)}), bf16[64,4,3584]{2,1,0:T(4,128)(2,1)S(1)}, u32[]{:S(2)}, u32[]{:S(2)}) %all-to-all-start.3) | async-done | bytes 1835040 | tf_op jit(solution)/shard_map/all_to_all | solution.py:62
  262.9 1.7 convert_add_fusion
  264.6 1.9 add.124
  266.5 0.9 gather_fusion.3
  267.4 0.2 fusion.13
  267.6 0.8 slice_bitcast_fusion.4
  (20 shorter events, 0.2 us)
Async XLA Ops:
  0.6 88.9 %copy-start = (bf16[1,3584,32]{1,2,0:T(8,128)(2,1)S(1)}, bf16[1,3584,32]{1,2,0:T(8,128)(2,1)}, u32[]{:S(2)}) copy-start(bf16[1,3584,32]{1,2,0:T(8,128)(2,1)} %param.14) | copy-start | bytes 688132
  81.6 9.0 %copy-start.4 = (s32[1,2,1,64,1]{3,4,2,1,0:T(1,128)S(1)}, s32[1,2,1,64,1]{3,4,2,1,0:T(1,128)}, u32[]{:S(2)}) copy-start(s32[1,2,1,64,1]{3,4,2,1,0:T(1,128)} %param.15) | copy-start | bytes 1540
  81.6 51.5 %all-to-all-start.1 = ((bf16[64,4,3584]{2,1,0:T(4,128)(2,1)}), bf16[64,4,3584]{2,1,0:T(4,128)(2,1)S(1)}, u32[]{:S(2)}, u32[]{:S(2)}) async-start(bf16[64,4,3584]{2,1,0:T(4,128)(2,1)} %reshape.172), calls=%async_computation.1 | async-start | bytes 3670016 | tf_op jit(solution)/shard_map/all_to_all | solution.py:62
  136.8 0.9 copy-start.1
  136.8 1.0 copy-start.2
  137.8 10.2 %copy-start.3 = (bf16[2,1,32,3584]{3,2,1,0:T(8,128)(2,1)S(1)}, bf16[2,1,32,3584]{3,2,1,0:T(8,128)(2,1)}, u32[]{:S(2)}) copy-start(bf16[2,1,32,3584]{3,2,1,0:T(8,128)(2,1)} %param.12) | copy-start | bytes 1376260
  138.1 6.2 %collective-permute-start = (bf16[32,3584]{1,0:T(8,128)(2,1)S(1)}, bf16[32,3584]{1,0:T(8,128)(2,1)S(1)}, u32[]{:S(2)}, u32[]{:S(2)}) collective-permute-start(bf16[32,3584]{1,0:T(8,128)(2,1)S(1)} %get-tuple-element.7), channel_id=1, source_target_pairs={{0,64},{64,128},{128,192},{192,256},{256,320},{320,384},{384,448},... | collective-permute-start | bytes 688136 | tf_op jit(solution)/shard_map/ppermute | solution.py:17
  139.4 8.7 %collective-permute-start.1 = (bf16[32,3584]{1,0:T(8,128)(2,1)S(1)}, bf16[32,3584]{1,0:T(8,128)(2,1)S(1)}, u32[]{:S(2)}, u32[]{:S(2)}) collective-permute-start(bf16[32,3584]{1,0:T(8,128)(2,1)S(1)} %get-tuple-element.8), channel_id=1, source_target_pairs={{64,0},{128,64},{192,128},{256,192},{320,256},{384,320},{448,384},... | collective-permute-start | bytes 688136 | tf_op jit(solution)/shard_map/ppermute | solution.py:17
  211.5 51.4 %all-to-all-start.3 = ((bf16[64,4,3584]{2,1,0:T(4,128)(2,1)}), bf16[64,4,3584]{2,1,0:T(4,128)(2,1)S(1)}, u32[]{:S(2)}, u32[]{:S(2)}) async-start(bf16[64,4,3584]{2,1,0:T(4,128)(2,1)} %reshape.176), calls=%async_computation.3 | async-start | bytes 3670016 | tf_op jit(solution)/shard_map/all_to_all | solution.py:62
where the time goes:
time: 269 us; the launch traced here: 268 us
  blocking collectives  115 us (43%)
  waiting for transfers between devices  94 us (35%)
  local copies, waits for them, and re-layouts  21.8 us (8%)
  starting transfers between devices  14.9 us (6%)
  matrix products  12.3 us (5%)
  other arithmetic  9.75 us (4%)
    all_to_all x2, blocking collectives, layer_rows(): lax.all_to_all(outgoing, 'expert', split_axis=0, concat_axis=0, tiled=True)  115 us
    all_to_all x2, waiting for transfers between devices, layer_rows(): lax.all_to_all(partial_value.reshape(holder_count, capacity, width), 'exp...  86.8 us
    all_to_all x2, starting transfers between devices, layer_rows(): lax.all_to_all(partial_value.reshape(holder_count, capacity, width), 'exp...  12.2 us
    dot_general x2, matrix products, expert_part(): jnp.dot(hidden, w_out, preferred_element_type=jnp.float32)  11.8 us
    ppermute x2, waiting for transfers between devices, from_behind(): lax.ppermute(value, axis, [(source, source + steps) for source in range(l...  7.18 us
  transfers between devices with their start and end apart: 4, of which 4 were waited for; matrix products, arithmetic and copies ran while one was open for 1% of the time, Pallas kernels for 0%

commit v1 on v0

v1 whole, which is shorter than its diff:
```python
import functools

import jax
import jax.numpy as jnp
from jax import lax
from jax.experimental import pallas as pl
from jax.experimental.pallas import tpu as pltpu
from jax.sharding import PartitionSpec as P

STEPS = 2
ROUTE_SCALE = 2.5
NORM_EPS = 1e-06

NX, NY = 4, 8
CHIPS = NX * NY
CAP = 4
CHUNK = 512
GROUPS = 2
LAG = 2
MESH = pl.DeviceIdType.MESH
BF16 = jnp.bfloat16
F32 = jnp.float32

OFFSETS = [(dx, dy) for dx in range(NX) for dy in range(NY)]


def hops(offset):
    return min(offset[0], NX - offset[0]) + min(offset[1], NY - offset[1])


def window_kernel(
    up_ref, down_ref, entering_ref, gain_ref, router_ref, routes_ref, w_in_ref, w_out_ref,
    up_out, down_out,
    w_in, w_out, rows, sent, got, made, back, hop_sent, hop_got, acc, hidden, spare,
    in_sem, out_sem, wsend_sem, sent_sem, got_sem, made_sem, back_sem, hop_send_sem, hop_sem,
):
    tok, width = up_ref.shape
    row_count = 2 * tok
    chunks = width // CHUNK
    slots = CHIPS * CAP
    group_rows = slots // GROUPS
    group_offsets = CHIPS // GROUPS

    section = lax.axis_index("pipe")
    last_section = lax.axis_size("pipe") - 1
    place = lax.axis_index("expert")
    core = place % 2
    chip_x = (place // 2) // NY
    chip_y = (place // 2) % NY
    partner = place + 1 - 2 * core
    above = lax.rem(section + 1, last_section + 1)
    below = lax.rem(section + last_section, last_section + 1)

    def peer(dx, dy, sign):
        x = (chip_x + sign * dx + NX) % NX
        y = (chip_y + sign * dy + NY) % NY
        return (x * NY + y) * 2 + core

    def columns(c):
        return pl.ds(pl.multiple_of(c * CHUNK, CHUNK), CHUNK)

    def local_weights(c, _):
        pltpu.make_async_copy(w_in_ref.at[columns(c)], w_in.at[core, columns(c)], in_sem.at[c]).start()
        pltpu.make_async_copy(
            w_out_ref.at[:, columns(c)], w_out.at[core, :, columns(c)], out_sem.at[c]
        ).start()
        return 0

    lax.fori_loop(0, chunks, local_weights, 0)

    barrier = pltpu.get_barrier_semaphore()
    for dx, dy in sorted(OFFSETS[1:], key=hops, reverse=True):
        pl.semaphore_signal(
            barrier, inc=1, device_id={"expert": peer(dx, dy, 1)}, device_id_type=MESH
        )
    for target in (above, below):
        pl.semaphore_signal(barrier, inc=1, device_id={"pipe": target}, device_id_type=MESH)
    pl.semaphore_signal(barrier, inc=1, device_id={"expert": partner}, device_id_type=MESH)

    def route(step):
        ids = routes_ref[step]
        member = (
            ids == lax.broadcasted_iota(jnp.int32, (row_count, CHIPS), 1)
        ).astype(F32)
        earlier = (
            lax.broadcasted_iota(jnp.int32, (row_count, row_count), 1)
            < lax.broadcasted_iota(jnp.int32, (row_count, row_count), 0)
        ).astype(F32)
        ranks = jnp.dot(earlier.astype(BF16), member.astype(BF16), preferred_element_type=F32)
        rank = jnp.sum(ranks * member, axis=1, keepdims=True).astype(jnp.int32)
        far_x = (lax.div(ids, NY) - chip_x + NX) & (NX - 1)
        far_y = ((ids & (NY - 1)) - chip_y + NY) & (NY - 1)
        slot = (far_x * NY + far_y) * CAP + rank
        place_row = (slot == lax.broadcasted_iota(jnp.int32, (row_count, slots), 1)).astype(F32)
        return member, place_row.astype(BF16), jnp.transpose(place_row).astype(BF16)

    plans = [route(step) for step in range(STEPS)]

    def admit(step, c, carry, chunk_rows):
        square, scores = carry
        rows[step, c] = chunk_rows
        values = chunk_rows.astype(F32)
        square = square + jnp.sum(values * values, axis=1, keepdims=True)
        scaled = (values * gain_ref[:, columns(c)]).astype(BF16)
        scores = scores + jnp.dot(scaled, router_ref[columns(c)], preferred_element_type=F32)
        sent[step, c] = jnp.dot(plans[step][2], chunk_rows, preferred_element_type=F32).astype(BF16)
        return square, scores

    def dispatch(step, group, c):
        for k in range(group * group_offsets, (group + 1) * group_offsets):
            mine = sent.at[step, c, pl.ds(CAP * k, CAP)]
            theirs = got.at[step, c, pl.ds(CAP * k, CAP)]
            if k == 0:
                pltpu.make_async_copy(mine, theirs, got_sem.at[step, group, c]).start()
                pltpu.make_async_copy(
                    mine, spare.at[2 * step, c, pl.ds(0, CAP)], sent_sem.at[step]
                ).start()
                continue
            pltpu.make_async_remote_copy(
                src_ref=mine,
                dst_ref=theirs,
                send_sem=sent_sem.at[step],
                recv_sem=got_sem.at[step, group, c],
                device_id={"expert": peer(*OFFSETS[k], 1)},
                device_id_type=MESH,
            ).start()

    def give_back(step, group, c):
        for k in range(group * group_offsets, (group + 1) * group_offsets):
            mine = made.at[step, c, pl.ds(CAP * k, CAP)]
            theirs = back.at[step, c, pl.ds(CAP * k, CAP)]
            if k == 0:
                pltpu.make_async_copy(mine, theirs, back_sem.at[step, group, c]).start()
                pltpu.make_async_copy(
                    mine, spare.at[2 * step + 1, c, pl.ds(0, CAP)], made_sem.at[step]
                ).start()
                continue
            pltpu.make_async_remote_copy(
                src_ref=mine,
                dst_ref=theirs,
                send_sem=made_sem.at[step],
                recv_sem=back_sem.at[step, group, c],
                device_id={"expert": peer(*OFFSETS[k], -1)},
                device_id_type=MESH,
            ).start()

    def wait_bytes(ref, sem):
        pltpu.make_async_copy(ref, ref, sem).wait()

    def experts(step, group):
        own = pl.ds(group * group_rows, group_rows)
        acc[...] = jnp.zeros_like(acc)

        def enter(c, square):
            wait_bytes(got.at[step, c, own], got_sem.at[step, group, c])
            if step == 0 and group == 0:
                wait_bytes(w_in.at[:, columns(c)], in_sem.at[c])
            values = got[step, c, own].astype(F32)
            square = square + jnp.sum(values * values, axis=1, keepdims=True)
            scaled = (values * gain_ref[:, columns(c)]).astype(BF16)
            for half in range(2):
                acc[half] += jnp.dot(scaled, w_in[half, columns(c)], preferred_element_type=F32)
            return square

        square = lax.fori_loop(0, chunks, enter, jnp.zeros((group_rows, 1), F32))
        factor = lax.rsqrt(square * (1.0 / width) + NORM_EPS)
        for half in range(2):
            hidden[half] = jax.nn.silu(acc[half] * factor).astype(BF16)

        def leave(c, _):
            if step == 0 and group == 0:
                wait_bytes(w_out.at[:, :, columns(c)], out_sem.at[c])
            total = jnp.dot(hidden[0], w_out[0, :, columns(c)], preferred_element_type=F32)
            total += jnp.dot(hidden[1], w_out[1, :, columns(c)], preferred_element_type=F32)
            made[step, c, own] = total.astype(BF16)
            give_back(step, group, c)
            return 0

        lax.fori_loop(0, chunks, leave, 0)

    def gate_of(step, carry):
        square, scores = carry
        factor = lax.rsqrt(square * (1.0 / width) + NORM_EPS)
        weights = jax.nn.sigmoid(scores * factor)
        return ROUTE_SCALE * jnp.sum(weights * plans[step][0], axis=1, keepdims=True)

    def combine(step, c, gate):
        for group in range(GROUPS):
            own = pl.ds(group * group_rows, group_rows)
            wait_bytes(back.at[step, c, own], back_sem.at[step, group, c])
        chosen = jnp.dot(plans[step][1], back[step, c], preferred_element_type=F32)
        return (rows[step, c].astype(F32) + gate * chosen).astype(BF16)

    empty = (jnp.zeros((row_count, 1), F32), jnp.zeros((row_count, CHIPS), F32))

    def first_rows(c, carry):
        chunk_rows = jnp.concatenate([up_ref[:, columns(c)], down_ref[:, columns(c)]], axis=0)
        return admit(0, c, carry, chunk_rows)

    carry = lax.fori_loop(0, chunks, first_rows, empty)

    pl.semaphore_wait(barrier, CHIPS + 2)

    def push_in(c, _):
        pltpu.make_async_remote_copy(
            src_ref=w_in_ref.at[columns(c)],
            dst_ref=w_in.at[core, columns(c)],
            send_sem=wsend_sem.at[0],
            recv_sem=in_sem.at[c],
            device_id={"expert": partner},
            device_id_type=MESH,
        ).start()
        return 0

    def push_out(c, _):
        pltpu.make_async_remote_copy(
            src_ref=w_out_ref.at[:, columns(c)],
            dst_ref=w_out.at[core, :, columns(c)],
            send_sem=wsend_sem.at[1],
            recv_sem=out_sem.at[c],
            device_id={"expert": partner},
            device_id_type=MESH,
        ).start()
        return 0

    def send_group(step, group):
        def one(c, _):
            dispatch(step, group, c)
            return 0

        lax.fori_loop(0, chunks, one, 0)

    send_group(0, 0)
    lax.fori_loop(0, chunks, push_in, 0)
    send_group(0, 1)
    lax.fori_loop(0, chunks, push_out, 0)

    for step in range(STEPS):
        gate = gate_of(step, carry)
        for group in range(GROUPS):
            experts(step, group)
        if step + 1 < STEPS:

            def relay(c):
                hop_sent[step, c] = combine(step, c, gate)
                for half, target in ((0, above), (1, below)):
                    part = pl.ds(half * tok, tok)
                    pltpu.make_async_remote_copy(
                        src_ref=hop_sent.at[step, c, part],
                        dst_ref=hop_got.at[step, c, part],
                        send_sem=hop_send_sem.at[step],
                        recv_sem=hop_sem.at[step, c],
                        device_id={"pipe": target},
                        device_id_type=MESH,
                    ).start()

            def take(c, carry):
                wait_bytes(hop_got.at[step, c], hop_sem.at[step, c])
                upward = jnp.where(
                    section == 0, entering_ref[0, step, :, columns(c)], hop_got[step, c, pl.ds(0, tok)]
                )
                downward = jnp.where(
                    section == last_section,
                    entering_ref[1, step, :, columns(c)],
                    hop_got[step, c, pl.ds(tok, tok)],
                )
                carry = admit(step + 1, c, carry, jnp.concatenate([upward, downward], axis=0))
                dispatch(step + 1, 0, c)
                return carry

            def head(c, _):
                relay(c)
                return 0

            def middle(c, carry):
                relay(c)
                return take(c - LAG, carry)

            lax.fori_loop(0, LAG, head, 0)
            carry = lax.fori_loop(LAG, chunks, middle, empty)
            carry = lax.fori_loop(chunks - LAG, chunks, take, carry)
            for group in range(1, GROUPS):
                send_group(step + 1, group)
        else:

            def finish(c, _):
                result = combine(step, c, gate)
                up_out[:, columns(c)] = result[:tok]
                down_out[:, columns(c)] = result[tok:]
                return 0

            lax.fori_loop(0, chunks, finish, 0)

    for step in range(STEPS):
        wait_bytes(sent.at[step], sent_sem.at[step])
        wait_bytes(made.at[step], made_sem.at[step])
        if step + 1 < STEPS:
            wait_bytes(hop_sent.at[step], hop_send_sem.at[step])
    wait_bytes(w_in.at[core], wsend_sem.at[0])
    wait_bytes(w_out.at[core], wsend_sem.at[1])


def shards(up_state, down_state, entering, norm_gain, router, routes, w_in, w_out):
    tok, width = up_state.shape[1:]
    half_units = w_in.shape[1]
    chunks = width // CHUNK
    slots = CHIPS * CAP
    vmem = pl.BlockSpec(memory_space=pltpu.VMEM)
    hbm = pl.BlockSpec(memory_space=pl.ANY)
    dma = pltpu.SemaphoreType.DMA
    blocks = pltpu.VMEM((STEPS, chunks, slots, CHUNK), BF16)
    up_new, down_new = pl.pallas_call(
        window_kernel,
        name="relay_window",
        out_shape=(
            jax.ShapeDtypeStruct((tok, width), BF16),
            jax.ShapeDtypeStruct((tok, width), BF16),
        ),
        in_specs=[vmem] * 6 + [hbm] * 2,
        out_specs=(vmem, vmem),
        scratch_shapes=[
            pltpu.VMEM((2, width, half_units), BF16),
            pltpu.VMEM((2, half_units, width), BF16),
            pltpu.VMEM((STEPS, chunks, 2 * tok, CHUNK), BF16),
            blocks,
            blocks,
            blocks,
            blocks,
            pltpu.VMEM((STEPS - 1, chunks, 2 * tok, CHUNK), BF16),
            pltpu.VMEM((STEPS - 1, chunks, 2 * tok, CHUNK), BF16),
            pltpu.VMEM((2, slots // GROUPS, half_units), F32),
            pltpu.VMEM((2, slots // GROUPS, half_units), BF16),
            pltpu.VMEM((2 * STEPS, chunks, 8, CHUNK), BF16),
            dma((chunks,)),
            dma((chunks,)),
            dma((2,)),
            dma((STEPS,)),
            dma((STEPS, GROUPS, chunks)),
            dma((STEPS,)),
            dma((STEPS, GROUPS, chunks)),
            dma((STEPS - 1,)),
            dma((STEPS - 1, chunks)),
        ],
        compiler_params=pltpu.CompilerParams(
            collective_id=0, has_side_effects=True, vmem_limit_bytes=60 * 2**20
        ),
    )(
        up_state[0],
        down_state[0],
        entering,
        norm_gain,
        router[0],
        routes[0, :, 0],
        w_in,
        w_out,
    )
    return (up_new[None], down_new[None])


def solution(mesh):
    return jax.shard_map(
        shards,
        mesh=mesh,
        in_specs=(
            P("pipe", "expert", None),
            P("pipe", "expert", None),
            P(None, None, "expert", None),
            P("pipe", None),
            P("pipe", None, None),
            P("pipe", None, "expert", None, None),
            P(None, "expert"),
            P("expert", None),
        ),
        out_specs=(P("pipe", "expert", None), P("pipe", "expert", None)),
        check_vma=False,
    )
```

time: 269 us -> 116 us (0.43)
  the two profiles are of different devices: /device:TPU:1 before, /device:TPU:8 now
where the time goes in v1:
time: 116 us
  Pallas kernels  108 us (93%)
  local copies, waits for them, and re-layouts  6.88 us (6%)
    pallas_call x1, Pallas kernels, shards(): pl.pallas_call(window_kernel, name='relay_window', out_shape=(jax.ShapeDt...  108 us
    unnamed x3, local copies, waits for them, and re-layouts  5.46 us

profile of v1, /device:TPU:8, one launch (start us, length us, event | category | flops | bytes accessed | tf_op | source)
XLA Modules:
  0.0 116.0 jit_solution(7015930763054371304)
XLA Ops:
  0.6 1.4 %copy.11.routes_ref = s32[2,64,1]{2,1,0:T(8,128)} copy(s32[2,64,1]{1,0,2:T(2,128)} %bitcast.11) | data formatting | bytes 1024 | tf_op jit(solution)/shard_map/squeeze | solution.py:353
  2.0 2.2 %copy.10 = bf16[1,3584,32]{2,1,0:T(8,128)(2,1)} copy(bf16[1,3584,32]{1,2,0:T(8,128)(2,1)} %param.12) | data formatting | bytes 458752 | tf_op args[4]
  4.2 108.5 %relay_window.1 = (bf16[32,3584]{1,0:T(8,128)(2,1)}, bf16[32,3584]{1,0:T(8,128)(2,1)}) custom-call(bf16[32,3584]{1,0:T(8,128)(2,1)} %bitcast.9, bf16[32,3584]{1,0:T(8,128)(2,1)} %bitcast.10, bf16[2,1,32,3584]{3,2,1,0:T(8,128)(2,1)} %entering_ref.1, f32[1,3584]{1,0:T(1,128)} %gain_ref.1, bf16[3584,32]{1,0:T(8,128)(2,1)} %bitcast.6, ...), custom_call_target="tpu_custom_call" | custom-call | tf_op jit(solution)/shard_map/relay_window/pallas_call | solution.py:312
  112.7 1.6 %copy.14 = bf16[1,32,3584]{2,1,0:T(8,128)(2,1)} copy(bf16[1,32,3584]{2,1,0:T(8,128)(2,1)} %bitcast.8) | data formatting | bytes 458752
  114.3 1.6 %copy.15 = bf16[1,32,3584]{2,1,0:T(8,128)(2,1)} copy(bf16[1,32,3584]{2,1,0:T(8,128)(2,1)} %bitcast.7) | data formatting | bytes 458752

commit v2 on v1

--- a/solution.py
+++ b/solution.py
@@ -31,8 +31,9 @@
 def window_kernel(
     up_ref, down_ref, entering_ref, gain_ref, router_ref, routes_ref, w_in_ref, w_out_ref,
     up_out, down_out,
-    w_in, w_out, rows, sent, got, made, back, hop_sent, hop_got, acc, hidden, spare,
+    start, entering, router, w_in, w_out, rows, sent, got, made, back, hop_sent, hop_got, acc, hidden, spare,
     in_sem, out_sem, wsend_sem, sent_sem, got_sem, made_sem, back_sem, hop_send_sem, hop_sem,
+    load_sem,
 ):
     tok, width = up_ref.shape
     row_count = 2 * tok
@@ -66,8 +67,6 @@
         ).start()
         return 0
 
-    lax.fori_loop(0, chunks, local_weights, 0)
-
     barrier = pltpu.get_barrier_semaphore()
     for dx, dy in sorted(OFFSETS[1:], key=hops, reverse=True):
         pl.semaphore_signal(
@@ -77,22 +76,30 @@
         pl.semaphore_signal(barrier, inc=1, device_id={"pipe": target}, device_id_type=MESH)
     pl.semaphore_signal(barrier, inc=1, device_id={"expert": partner}, device_id_type=MESH)
 
+    loads = [
+        pltpu.make_async_copy(up_ref, start.at[pl.ds(0, tok)], load_sem.at[0]),
+        pltpu.make_async_copy(down_ref, start.at[pl.ds(tok, tok)], load_sem.at[1]),
+        pltpu.make_async_copy(router_ref, router, load_sem.at[2]),
+        pltpu.make_async_copy(entering_ref, entering, load_sem.at[3]),
+    ]
+    for load in loads:
+        load.start()
+    lax.fori_loop(0, chunks, local_weights, 0)
+
     def route(step):
-        ids = routes_ref[step]
-        member = (
-            ids == lax.broadcasted_iota(jnp.int32, (row_count, CHIPS), 1)
+        ids = routes_ref[pl.ds(step, 1)]
+        member = (ids == lax.broadcasted_iota(jnp.int32, (CHIPS, row_count), 0)).astype(F32)
+        earlier = (
+            lax.broadcasted_iota(jnp.int32, (row_count, row_count), 0)
+            < lax.broadcasted_iota(jnp.int32, (row_count, row_count), 1)
         ).astype(F32)
-        earlier = (
-            lax.broadcasted_iota(jnp.int32, (row_count, row_count), 1)
-            < lax.broadcasted_iota(jnp.int32, (row_count, row_count), 0)
-        ).astype(F32)
-        ranks = jnp.dot(earlier.astype(BF16), member.astype(BF16), preferred_element_type=F32)
-        rank = jnp.sum(ranks * member, axis=1, keepdims=True).astype(jnp.int32)
+        ranks = jnp.dot(member.astype(BF16), earlier.astype(BF16), preferred_element_type=F32)
+        rank = jnp.sum(ranks * member, axis=0, keepdims=True).astype(jnp.int32)
         far_x = (lax.div(ids, NY) - chip_x + NX) & (NX - 1)
         far_y = ((ids & (NY - 1)) - chip_y + NY) & (NY - 1)
         slot = (far_x * NY + far_y) * CAP + rank
-        place_row = (slot == lax.broadcasted_iota(jnp.int32, (row_count, slots), 1)).astype(F32)
-        return member, place_row.astype(BF16), jnp.transpose(place_row).astype(BF16)
+        holds = (slot == lax.broadcasted_iota(jnp.int32, (slots, row_count), 0)).astype(F32)
+        return jnp.transpose(member), jnp.transpose(holds).astype(BF16), holds.astype(BF16)
 
     plans = [route(step) for step in range(STEPS)]
 
@@ -102,7 +109,9 @@
         values = chunk_rows.astype(F32)
         square = square + jnp.sum(values * values, axis=1, keepdims=True)
         scaled = (values * gain_ref[:, columns(c)]).astype(BF16)
-        scores = scores + jnp.dot(scaled, router_ref[columns(c)], preferred_element_type=F32)
+        scores = scores + lax.dot_general(
+            scaled, router[:, columns(c)], (((1,), (1,)), ((), ())), preferred_element_type=F32
+        )
         sent[step, c] = jnp.dot(plans[step][2], chunk_rows, preferred_element_type=F32).astype(BF16)
         return square, scores
 
@@ -194,9 +203,10 @@
     empty = (jnp.zeros((row_count, 1), F32), jnp.zeros((row_count, CHIPS), F32))
 
     def first_rows(c, carry):
-        chunk_rows = jnp.concatenate([up_ref[:, columns(c)], down_ref[:, columns(c)]], axis=0)
-        return admit(0, c, carry, chunk_rows)
-
+        return admit(0, c, carry, start[:, columns(c)])
+
+    for load in loads[:3]:
+        load.wait()
     carry = lax.fori_loop(0, chunks, first_rows, empty)
 
     pl.semaphore_wait(barrier, CHIPS + 2)
@@ -232,7 +242,8 @@
 
     send_group(0, 0)
     lax.fori_loop(0, chunks, push_in, 0)
-    send_group(0, 1)
+    for group in range(1, GROUPS):
+        send_group(0, group)
     lax.fori_loop(0, chunks, push_out, 0)
 
     for step in range(STEPS):
@@ -240,6 +251,8 @@
         for group in range(GROUPS):
             experts(step, group)
         if step + 1 < STEPS:
+            if step == 0:
+                loads[3].wait()
 
             def relay(c):
                 hop_sent[step, c] = combine(step, c, gate)
@@ -257,11 +270,11 @@
             def take(c, carry):
                 wait_bytes(hop_got.at[step, c], hop_sem.at[step, c])
                 upward = jnp.where(
-                    section == 0, entering_ref[0, step, :, columns(c)], hop_got[step, c, pl.ds(0, tok)]
+                    section == 0, entering[0, step, :, columns(c)], hop_got[step, c, pl.ds(0, tok)]
                 )
                 downward = jnp.where(
                     section == last_section,
-                    entering_ref[1, step, :, columns(c)],
+                    entering[1, step, :, columns(c)],
                     hop_got[step, c, pl.ds(tok, tok)],
                 )
                 carry = admit(step + 1, c, carry, jnp.concatenate([upward, downward], axis=0))
@@ -300,13 +313,18 @@
     wait_bytes(w_out.at[core], wsend_sem.at[1])
 
 
+def hand_over(up_ref, down_ref, up_out, down_out):
+    up_out[...] = up_ref[...]
+    down_out[...] = down_ref[...]
+
+
 def shards(up_state, down_state, entering, norm_gain, router, routes, w_in, w_out):
     tok, width = up_state.shape[1:]
     half_units = w_in.shape[1]
     chunks = width // CHUNK
     slots = CHIPS * CAP
     vmem = pl.BlockSpec(memory_space=pltpu.VMEM)
-    hbm = pl.BlockSpec(memory_space=pl.ANY)
+    hbm = pl.BlockSpec(memory_space=pltpu.HBM)
     dma = pltpu.SemaphoreType.DMA
     blocks = pltpu.VMEM((STEPS, chunks, slots, CHUNK), BF16)
     up_new, down_new = pl.pallas_call(
@@ -316,9 +334,12 @@
             jax.ShapeDtypeStruct((tok, width), BF16),
             jax.ShapeDtypeStruct((tok, width), BF16),
         ),
-        in_specs=[vmem] * 6 + [hbm] * 2,
+        in_specs=[hbm] * 3 + [vmem, hbm, vmem] + [hbm] * 2,
         out_specs=(vmem, vmem),
         scratch_shapes=[
+            pltpu.VMEM((2 * tok, width), BF16),
+            pltpu.VMEM(entering.shape, BF16),
+            pltpu.VMEM((CHIPS, width), BF16),
             pltpu.VMEM((2, width, half_units), BF16),
             pltpu.VMEM((2, half_units, width), BF16),
             pltpu.VMEM((STEPS, chunks, 2 * tok, CHUNK), BF16),
@@ -340,6 +361,7 @@
             dma((STEPS, GROUPS, chunks)),
             dma((STEPS - 1,)),
             dma((STEPS - 1, chunks)),
+            dma((4,)),
         ],
         compiler_params=pltpu.CompilerParams(
             collective_id=0, has_side_effects=True, vmem_limit_bytes=60 * 2**20
@@ -349,11 +371,19 @@
         down_state[0],
         entering,
         norm_gain,
-        router[0],
-        routes[0, :, 0],
+        router[0].T,
+        routes[0, :, 0, :, 0],
         w_in,
         w_out,
     )
+    result = jax.ShapeDtypeStruct((tok, width), BF16)
+    up_new, down_new = pl.pallas_call(
+        hand_over,
+        name="hand_over",
+        out_shape=(result, result),
+        in_specs=[vmem, vmem],
+        out_specs=(vmem, vmem),
+    )(up_new, down_new)
     return (up_new[None], down_new[None])
 
 

time: 116 us -> 111 us (0.957)
  local copies, waits for them, and re-layouts: 6.88 us -> 0 us
  Pallas kernels: 108 us -> 110 us
    unnamed x3 -> x0, local copies, waits for them, and re-layouts: 5.46 us -> none
    pallas_call x0 -> x1, Pallas kernels: none -> 1.83 us  [shards(): pl.pallas_call(hand_over, name='hand_over', out_shape=(result, result), i...]
    squeeze x1 -> x0, local copies, waits for them, and re-layouts: 1.41 us -> none  [shards(): routes[0, :, 0]]
where the time goes in v2:
time: 111 us
  Pallas kernels  110 us (99%)
    pallas_call x1, Pallas kernels, shards(): pl.pallas_call(window_kernel, name='relay_window', out_shape=(jax.ShapeDt...  108 us

profile of v2, /device:TPU:8, one launch (start us, length us, event | category | flops | bytes accessed | tf_op | source)
XLA Modules:
  0.0 110.5 jit_solution(17690704521398520807)
XLA Ops:
  0.6 108.0 %relay_window.1 = (bf16[32,3584]{1,0:T(8,128)(2,1)}, bf16[32,3584]{1,0:T(8,128)(2,1)}) custom-call(bf16[32,3584]{1,0:T(8,128)(2,1)} %bitcast.8, bf16[32,3584]{1,0:T(8,128)(2,1)} %bitcast.9, bf16[2,1,32,3584]{3,2,1,0:T(8,128)(2,1)} %entering_ref.1, f32[1,3584]{1,0:T(1,128)} %gain_ref.1, bf16[32,3584]{1,0:T(8,128)(2,1)} %bitcast.10, s32[2,64]{1,0:T(2,128)} %bitcast.11, ...), custom_call_target="tpu_custom_call" | custom-call | tf_op jit(solution)/shard_map/relay_window/pallas_call | solution.py:330
  108.7 1.8 %hand_over.1 = (bf16[32,3584]{1,0:T(8,128)(2,1)}, bf16[32,3584]{1,0:T(8,128)(2,1)}) custom-call(bf16[32,3584]{1,0:T(8,128)(2,1)} %get-tuple-element.6.up_ref, bf16[32,3584]{1,0:T(8,128)(2,1)} %get-tuple-element.7.down_ref), custom_call_target="tpu_custom_call" | custom-call | tf_op jit(solution)/shard_map/hand_over/pallas_call | solution.py:380

commit v3 on v2

--- a/solution.py
+++ b/solution.py
@@ -31,7 +31,7 @@
 def window_kernel(
     up_ref, down_ref, entering_ref, gain_ref, router_ref, routes_ref, w_in_ref, w_out_ref,
     up_out, down_out,
-    start, entering, router, w_in, w_out, rows, sent, got, made, back, hop_sent, hop_got, acc, hidden, spare,
+    start, router, w_in, w_out, rows, sent, got, made, back, hop_sent, hop_got, acc, hidden, spare,
     in_sem, out_sem, wsend_sem, sent_sem, got_sem, made_sem, back_sem, hop_send_sem, hop_sem,
     load_sem,
 ):
@@ -49,8 +49,11 @@
     chip_x = (place // 2) // NY
     chip_y = (place // 2) % NY
     partner = place + 1 - 2 * core
-    above = lax.rem(section + 1, last_section + 1)
-    below = lax.rem(section + last_section, last_section + 1)
+    above = section + 1
+    below = section - 1
+    neighbours = (section + last_section) // (last_section + 1) + (
+        2 * last_section - section
+    ) // (last_section + 1)
 
     def peer(dx, dy, sign):
         x = (chip_x + sign * dx + NX) % NX
@@ -72,19 +75,38 @@
         pl.semaphore_signal(
             barrier, inc=1, device_id={"expert": peer(dx, dy, 1)}, device_id_type=MESH
         )
-    for target in (above, below):
-        pl.semaphore_signal(barrier, inc=1, device_id={"pipe": target}, device_id_type=MESH)
+    for inside, target in ((section < last_section, above), (section > 0, below)):
+
+        @pl.when(inside)
+        def _(target=target):
+            pl.semaphore_signal(barrier, inc=1, device_id={"pipe": target}, device_id_type=MESH)
+
     pl.semaphore_signal(barrier, inc=1, device_id={"expert": partner}, device_id_type=MESH)
 
     loads = [
         pltpu.make_async_copy(up_ref, start.at[pl.ds(0, tok)], load_sem.at[0]),
         pltpu.make_async_copy(down_ref, start.at[pl.ds(tok, tok)], load_sem.at[1]),
         pltpu.make_async_copy(router_ref, router, load_sem.at[2]),
-        pltpu.make_async_copy(entering_ref, entering, load_sem.at[3]),
     ]
     for load in loads:
         load.start()
     lax.fori_loop(0, chunks, local_weights, 0)
+
+    for side, at_edge in ((0, section == 0), (1, section == last_section)):
+
+        @pl.when(at_edge)
+        def _(side=side):
+            for step in range(STEPS - 1):
+
+                def enter_edge(c, _):
+                    pltpu.make_async_copy(
+                        entering_ref.at[side, step, :, columns(c)],
+                        hop_got.at[step, c, pl.ds(side * tok, tok)],
+                        hop_sem.at[step, c],
+                    ).start()
+                    return 0
+
+                lax.fori_loop(0, chunks, enter_edge, 0)
 
     def route(step):
         ids = routes_ref[pl.ds(step, 1)]
@@ -205,11 +227,11 @@
     def first_rows(c, carry):
         return admit(0, c, carry, start[:, columns(c)])
 
-    for load in loads[:3]:
+    for load in loads:
         load.wait()
     carry = lax.fori_loop(0, chunks, first_rows, empty)
 
-    pl.semaphore_wait(barrier, CHIPS + 2)
+    pl.semaphore_wait(barrier, CHIPS + neighbours)
 
     def push_in(c, _):
         pltpu.make_async_remote_copy(
@@ -251,33 +273,30 @@
         for group in range(GROUPS):
             experts(step, group)
         if step + 1 < STEPS:
-            if step == 0:
-                loads[3].wait()
 
             def relay(c):
                 hop_sent[step, c] = combine(step, c, gate)
-                for half, target in ((0, above), (1, below)):
-                    part = pl.ds(half * tok, tok)
-                    pltpu.make_async_remote_copy(
-                        src_ref=hop_sent.at[step, c, part],
-                        dst_ref=hop_got.at[step, c, part],
-                        send_sem=hop_send_sem.at[step],
-                        recv_sem=hop_sem.at[step, c],
-                        device_id={"pipe": target},
-                        device_id_type=MESH,
-                    ).start()
+                for half, inside, target in (
+                    (0, section < last_section, above),
+                    (1, section > 0, below),
+                ):
+
+                    @pl.when(inside)
+                    def _(half=half, target=target):
+                        part = pl.ds(half * tok, tok)
+                        pltpu.make_async_remote_copy(
+                            src_ref=hop_sent.at[step, c, part],
+                            dst_ref=hop_got.at[step, c, part],
+                            send_sem=hop_send_sem.at[step, half],
+                            recv_sem=hop_sem.at[step, c],
+                            device_id={"pipe": target},
+                            device_id_type=MESH,
+                        ).start()
+
 
             def take(c, carry):
                 wait_bytes(hop_got.at[step, c], hop_sem.at[step, c])
-                upward = jnp.where(
-                    section == 0, entering[0, step, :, columns(c)], hop_got[step, c, pl.ds(0, tok)]
-                )
-                downward = jnp.where(
-                    section == last_section,
-                    entering[1, step, :, columns(c)],
-                    hop_got[step, c, pl.ds(tok, tok)],
-                )
-                carry = admit(step + 1, c, carry, jnp.concatenate([upward, downward], axis=0))
+                carry = admit(step + 1, c, carry, hop_got[step, c])
                 dispatch(step + 1, 0, c)
                 return carry
 
@@ -308,7 +327,13 @@
         wait_bytes(sent.at[step], sent_sem.at[step])
         wait_bytes(made.at[step], made_sem.at[step])
         if step + 1 < STEPS:
-            wait_bytes(hop_sent.at[step], hop_send_sem.at[step])
+            for half, inside in ((0, section < last_section), (1, section > 0)):
+
+                @pl.when(inside)
+                def _(step=step, half=half):
+                    part = pl.ds(half * tok, tok)
+                    wait_bytes(hop_sent.at[step, :, part], hop_send_sem.at[step, half])
+
     wait_bytes(w_in.at[core], wsend_sem.at[0])
     wait_bytes(w_out.at[core], wsend_sem.at[1])
 
@@ -338,7 +363,6 @@
         out_specs=(vmem, vmem),
         scratch_shapes=[
             pltpu.VMEM((2 * tok, width), BF16),
-            pltpu.VMEM(entering.shape, BF16),
             pltpu.VMEM((CHIPS, width), BF16),
             pltpu.VMEM((2, width, half_units), BF16),
             pltpu.VMEM((2, half_units, width), BF16),
@@ -359,9 +383,9 @@
             dma((STEPS, GROUPS, chunks)),
             dma((STEPS,)),
             dma((STEPS, GROUPS, chunks)),
-            dma((STEPS - 1,)),
+            dma((STEPS - 1, 2)),
             dma((STEPS - 1, chunks)),
-            dma((4,)),
+            dma((3,)),
         ],
         compiler_params=pltpu.CompilerParams(
             collective_id=0, has_side_effects=True, vmem_limit_bytes=60 * 2**20

time: 111 us -> 100 us (0.901)
  Pallas kernels: 110 us -> 99.4 us
    pallas_call x1, Pallas kernels: 108 us -> 97.6 us  [shards(): pl.pallas_call(window_kernel, name='relay_window', out_shape=(jax.ShapeDt...]
where the time goes in v3:
time: 100 us
  Pallas kernels  99.4 us (99%)
    pallas_call x1, Pallas kernels, shards(): pl.pallas_call(window_kernel, name='relay_window', out_shape=(jax.ShapeDt...  97.6 us

profile of v3, /device:TPU:8, one launch (start us, length us, event | category | flops | bytes accessed | tf_op | source)
XLA Modules:
  0.0 100.0 jit_solution(9758960900363903918)
XLA Ops:
  0.6 97.6 %relay_window.1 = (bf16[32,3584]{1,0:T(8,128)(2,1)}, bf16[32,3584]{1,0:T(8,128)(2,1)}) custom-call(bf16[32,3584]{1,0:T(8,128)(2,1)} %bitcast.8, bf16[32,3584]{1,0:T(8,128)(2,1)} %bitcast.9, bf16[2,1,32,3584]{3,2,1,0:T(8,128)(2,1)} %entering_ref.1, f32[1,3584]{1,0:T(1,128)} %gain_ref.1, bf16[32,3584]{1,0:T(8,128)(2,1)} %bitcast.10, s32[2,64]{1,0:T(2,128)} %bitcast.11, ...), custom_call_target="tpu_custom_call" | custom-call | tf_op jit(solution)/shard_map/relay_window/pallas_call | solution.py:355
  98.2 1.8 %hand_over.1 = (bf16[32,3584]{1,0:T(8,128)(2,1)}, bf16[32,3584]{1,0:T(8,128)(2,1)}) custom-call(bf16[32,3584]{1,0:T(8,128)(2,1)} %get-tuple-element.6.up_ref, bf16[32,3584]{1,0:T(8,128)(2,1)} %get-tuple-element.7.down_ref), custom_call_target="tpu_custom_call" | custom-call | tf_op jit(solution)/shard_map/hand_over/pallas_call | solution.py:404
